TPU v7x, 256 devices: a whole 4x4x8 slice. The times are simulated.
256 devices in a mesh: panel: 32 (over z, y_lo, core), rep: 8 (over x, y_hi).
Axes of the slice: x: 4, y: 4 (y_hi: 2, y_lo: 2; y = y_hi * 2 + y_lo), z: 8, core: 2. Of those that a mesh axis runs over, the one named last changes fastest.
Arguments:
- x_src: bfloat16 [4096, 128], P('panel'), may hold values from -6 to 6
- x_dst: bfloat16 [131072, 128], P(('panel', 'rep')), may hold values from -6 to 6
- weight: bfloat16 [128, 512], replicated, may hold values from -0.5 to 0.5
- att_src: float32 [8, 64], replicated, may hold values from -0.75 to 0.75
- att_dst: float32 [8, 64], replicated, may hold values from -0.75 to 0.75
- grad_out: bfloat16 [131072, 512], P(('panel', 'rep')), may hold values from -6 to 6
- block_rows: int32 [4096], P(('panel', 'rep')), may hold values from 0 to 3, as said below
- block_cols: int32 [4096], P(('panel', 'rep')), may hold values from 0 to 31
- block_masks: int32 [4096, 128, 128], P(('panel', 'rep')), may hold values from 0 to 1, as said below
- block_counts: int32 [256], P(('panel', 'rep')), may hold values from 2 to 16, as said below
Outputs:
- grad_src: float32 [4096, 128], P('panel')
- grad_dst: float32 [131072, 128], P(('panel', 'rep'))
- grad_weight: float32 [128, 512], replicated
- grad_att_src: float32 [8, 64], replicated
- grad_att_dst: float32 [8, 64], replicated
Inputs may be any that keep to these rules, and one draw needn't show every extreme that they name: `block_counts`: live block slots of one device; at least one device has exactly 16. The pairs of block_rows and block_cols within one device's 16 slots are distinct. `block_masks`: slots at or after a device's count of live blocks hold only zeros.
All inputs are finite; a program needn't handle non-finite values.
Results may differ from a plain program's by a relative error of at most 0.012.
The roundings to bfloat16 on the way count: a program that leaves them out, or rounds other values in their place, can miss the bound.
Values may be sent and summed in bfloat16 or wider, within the bound.
No kernel may reach another device: no remote copies, remote signals or barrier semaphores. Data moves between devices by JAX's collectives and lax.ppermute only.
A program may use at most 128 MiB of HBM per device.

v0:
```python
import math
import jax
import jax.numpy as jnp
from jax import lax
from jax.sharding import PartitionSpec as P

HIGHEST_PRECISION = lax.Precision.HIGHEST


def smooth_leaky(values):
    return 0.2 * values + 0.8 * jax.nn.softplus(values)


def smooth_slope(values):
    return 0.2 + 0.8 * jax.nn.sigmoid(values)


def shards(
    x_src,
    x_dst,
    weight,
    att_src,
    att_dst,
    grad_out,
    block_rows,
    block_cols,
    block_masks,
    block_counts,
):
    num_heads, head_dim = att_src.shape
    model_width = weight.shape[1]
    block_size = block_masks.shape[1]
    dest_count = x_dst.shape[0]
    source_local = x_src.shape[0]
    slot_count = block_rows.shape[0]
    proj_own = jnp.dot(x_src, weight, preferred_element_type=jnp.float32).astype(jnp.bfloat16)
    proj_all = lax.all_gather(proj_own, "panel", axis=0, tiled=True)
    source_total = proj_all.shape[0]
    dest_blocks = dest_count // block_size
    source_blocks = source_total // block_size
    source_feats = proj_all.reshape(source_total, num_heads, head_dim)
    score_src = jnp.einsum(
        "jhk,hk->hj", source_feats.astype(jnp.float32), att_src, precision=HIGHEST_PRECISION
    )
    proj_dst = jnp.dot(x_dst, weight, preferred_element_type=jnp.float32).astype(jnp.bfloat16)
    feats = proj_dst.reshape(dest_count, num_heads, head_dim)
    feats_wide = feats.astype(jnp.float32)
    score_d = jnp.einsum("ihk,hk->hi", feats_wide, att_dst, precision=HIGHEST_PRECISION)
    score_own = jnp.einsum("ihk,hk->hi", feats_wide, att_src, precision=HIGHEST_PRECISION)
    cotan = grad_out.reshape(dest_count, num_heads, head_dim)
    cotan_wide = cotan.astype(jnp.float32)
    live_count = block_counts[0]
    score_d_blocks = score_d.reshape(num_heads, dest_blocks, block_size)
    score_src_blocks = score_src.reshape(num_heads, source_blocks, block_size)
    source_row_blocks = source_feats.reshape(source_blocks, block_size, num_heads, head_dim)
    cotan_blocks = cotan.reshape(dest_blocks, block_size, num_heads, head_dim)
    group = math.gcd(slot_count, 16)
    groups = slot_count // group
    alive_all = (jnp.arange(slot_count, dtype=jnp.int32) < live_count).astype(jnp.float32)
    slot_inputs = (
        block_rows.reshape(groups, group),
        block_cols.reshape(groups, group),
        block_masks.reshape(groups, group, block_size, block_size),
        alive_all.reshape(groups, group),
    )

    def group_scores(rows, cols, masks, alive):
        dest_hot = (rows[:, None] == jnp.arange(dest_blocks, dtype=jnp.int32)[None, :]).astype(
            jnp.float32
        )
        source_hot = (cols[:, None] == jnp.arange(source_blocks, dtype=jnp.int32)[None, :]).astype(
            jnp.float32
        )
        score_rows = jnp.einsum(
            "gd,hdu->ghu", dest_hot, score_d_blocks, precision=HIGHEST_PRECISION
        )
        score_cols = jnp.einsum(
            "gs,hsv->ghv", source_hot, score_src_blocks, precision=HIGHEST_PRECISION
        )
        pre_score = score_rows[:, :, :, None] + score_cols[:, :, None, :]
        edge_mask = masks.astype(jnp.float32) * alive[:, None, None]
        edge_weight = jnp.exp(smooth_leaky(pre_score)) * edge_mask[:, None]
        source_rows = jnp.take(source_row_blocks, cols, axis=0)
        return (dest_hot, source_hot, pre_score, edge_weight, source_rows)

    def forward_group(carried_fwd, slot_group):
        denominator, numerator = carried_fwd
        rows, cols, masks, alive = slot_group
        dest_hot, source_hot, pre_score, edge_weight, source_rows = group_scores(
            rows, cols, masks, alive
        )
        part_num = jnp.einsum(
            "ghij,gjhk->gihk",
            edge_weight.astype(jnp.bfloat16),
            source_rows,
            preferred_element_type=jnp.float32,
        )
        denominator = denominator + jnp.einsum(
            "gd,ghi->hdi", dest_hot, edge_weight.sum(axis=3), precision=HIGHEST_PRECISION
        )
        numerator = numerator + jnp.einsum(
            "gd,gihk->dihk", dest_hot, part_num, precision=HIGHEST_PRECISION
        )
        return ((denominator, numerator), None)

    (denominator_blocks, numerator_blocks), _ = lax.scan(
        forward_group,
        (
            jnp.zeros((num_heads, dest_blocks, block_size), jnp.float32),
            jnp.zeros((dest_blocks, block_size, num_heads, head_dim), jnp.float32),
        ),
        slot_inputs,
    )
    denominator = denominator_blocks.reshape(num_heads, dest_count)
    numerator = numerator_blocks.reshape(dest_count, num_heads, head_dim)
    pre_self = score_d + score_own
    self_weight = jnp.exp(smooth_leaky(pre_self))
    denominator = denominator + self_weight
    numerator = numerator + self_weight.T[:, :, None] * feats_wide
    attended = numerator / denominator.T[:, :, None]
    centred = jnp.sum(cotan_wide * attended, axis=2).T
    denominator_full = denominator.reshape(num_heads, dest_blocks, block_size)
    centred_full = centred.reshape(num_heads, dest_blocks, block_size)

    def backward_group(carried_bwd, slot_group):
        grad_source, grad_score_src, grad_score_dst = carried_bwd
        rows, cols, masks, alive = slot_group
        dest_hot, source_hot, pre_score, edge_weight, source_rows = group_scores(
            rows, cols, masks, alive
        )
        denom_rows = jnp.einsum(
            "gd,hdi->ghi", dest_hot, denominator_full, precision=HIGHEST_PRECISION
        )
        attention = edge_weight / denom_rows[:, :, :, None]
        cotan_rows = jnp.take(cotan_blocks, rows, axis=0)
        pair_grad = jnp.einsum(
            "gihk,gjhk->ghij", cotan_rows, source_rows, preferred_element_type=jnp.float32
        )
        centred_rows = jnp.einsum(
            "gd,hdi->ghi", dest_hot, centred_full, precision=HIGHEST_PRECISION
        )
        score_grad = attention * (pair_grad - centred_rows[:, :, :, None]) * smooth_slope(pre_score)
        feat_grad = jnp.einsum(
            "ghij,gihk->gjhk",
            attention.astype(jnp.bfloat16),
            cotan_rows,
            preferred_element_type=jnp.float32,
        )
        grad_source = grad_source + jnp.einsum(
            "gs,gjhk->sjhk", source_hot, feat_grad, precision=HIGHEST_PRECISION
        )
        grad_score_src = grad_score_src + jnp.einsum(
            "gs,ghj->hsj", source_hot, score_grad.sum(axis=2), precision=HIGHEST_PRECISION
        )
        grad_score_dst = grad_score_dst + jnp.einsum(
            "gd,ghi->hdi", dest_hot, score_grad.sum(axis=3), precision=HIGHEST_PRECISION
        )
        return ((grad_source, grad_score_src, grad_score_dst), None)

    (grad_source_blocks, grad_score_src_blocks, grad_score_dst_blocks), _ = lax.scan(
        backward_group,
        (
            jnp.zeros((source_blocks, block_size, num_heads, head_dim), jnp.float32),
            jnp.zeros((num_heads, source_blocks, block_size), jnp.float32),
            jnp.zeros((num_heads, dest_blocks, block_size), jnp.float32),
        ),
        slot_inputs,
    )
    grad_source = grad_source_blocks.reshape(source_total, num_heads, head_dim)
    grad_score_src = grad_score_src_blocks.reshape(num_heads, source_total)
    grad_score_dst = grad_score_dst_blocks.reshape(num_heads, dest_count)
    self_attention = self_weight / denominator
    self_pair = jnp.sum(cotan_wide * feats_wide, axis=2).T
    self_grad = self_attention * (self_pair - centred) * smooth_slope(pre_self)
    grad_score_dst = grad_score_dst + self_grad
    grad_dest = (
        self_attention.T[:, :, None] * cotan_wide
        + self_grad.T[:, :, None] * att_src[None]
        + grad_score_dst.T[:, :, None] * att_dst[None]
    )
    grad_source = grad_source + grad_score_src.T[:, :, None] * att_src[None]
    att_src_part = jnp.einsum(
        "hj,jhk->hk", grad_score_src, source_feats.astype(jnp.float32), precision=HIGHEST_PRECISION
    ) + jnp.einsum("hi,ihk->hk", self_grad, feats_wide, precision=HIGHEST_PRECISION)
    att_dst_part = jnp.einsum("hi,ihk->hk", grad_score_dst, feats_wide, precision=HIGHEST_PRECISION)
    weight_t = weight.astype(jnp.float32).T
    source_flat = grad_source.reshape(source_total, model_width)
    dest_flat = grad_dest.reshape(dest_count, model_width)
    grad_dst = jnp.dot(dest_flat, weight_t, precision=HIGHEST_PRECISION)
    weight_part = jnp.dot(x_dst.astype(jnp.float32).T, dest_flat, precision=HIGHEST_PRECISION)
    share_rows = source_local // lax.axis_size("rep")
    share_start = lax.axis_index("rep") * share_rows
    panel_part = lax.psum_scatter(source_flat, "panel", scatter_dimension=0, tiled=True)
    panel_sum = lax.psum(panel_part, "rep")
    own_share = lax.dynamic_slice_in_dim(panel_sum, share_start, share_rows, 0)
    grad_src = jnp.dot(panel_sum, weight_t, precision=HIGHEST_PRECISION)
    own_inputs = lax.dynamic_slice_in_dim(x_src, share_start, share_rows, 0).astype(jnp.float32)
    weight_part = weight_part + jnp.dot(own_inputs.T, own_share, precision=HIGHEST_PRECISION)
    grad_weight, grad_att_src, grad_att_dst = lax.psum(
        (weight_part, att_src_part, att_dst_part), ("panel", "rep")
    )
    return (grad_src, grad_dst, grad_weight, grad_att_src, grad_att_dst)


def solution(mesh):
    return jax.shard_map(
        shards,
        mesh=mesh,
        in_specs=(
            P("panel", None),
            P(("panel", "rep"), None),
            P(),
            P(),
            P(),
            P(("panel", "rep"), None),
            P(("panel", "rep")),
            P(("panel", "rep")),
            P(("panel", "rep"), None, None),
            P(("panel", "rep")),
        ),
        out_specs=(P("panel", None), P(("panel", "rep"), None), P(), P(), P()),
        check_vma=False,
    )
```

profile of v0, /device:TPU:2, one launch (start us, length us, event | category | flops | bytes accessed | tf_op | source)
XLA Modules:
  0.0 674.6 jit_solution(18316904664663348412)
XLA Ops:
  7.2 0.0 copy-start
  7.2 0.0 copy-start.7
  7.2 0.0 copy-start.6
  7.2 0.0 all-gather.2.cloned.1.call-start
  7.3 0.8 copy-done
  8.1 1.6 convolution_convert_fusion.1
  9.7 0.0 all-gather.2.cloned.1.call-update
  9.7 0.0 reduce-scatter.2.cloned.1.call-start
  9.7 2.1 copy.48
  11.8 1.6 reshape.148
  13.4 1.2 convolution_convert_fusion
  14.7 1.0 fusion.98
  15.7 0.9 fusion.94
  17.3 0.6 copy.39
  17.9 0.8 mul.185
  18.7 0.7 compare_select_fusion.3
  19.4 0.9 gather_fusion
  20.3 0.0 copy-done.9
  20.4 0.3 fusion.100
  20.7 2.4 convert_multiply_fusion.2
  23.1 57.2 %all-gather.2.cloned.1.call-done = bf16[4096,512]{1,0:T(8,128)(2,1)} async-done(((bf16[128,512]{1,0:T(8,128)(2,1)}), bf16[4096,512]{1,0:T(8,128)(2,1)}) %all-gather.2.cloned.1.call-update) | async-done | bytes 4194320 | tf_op jit(solution)/shard_map/all_gather | solution.py:37
  80.3 6.4 copy.41
  86.7 3.9 fusion.99
  90.6 0.1 copy.113
  90.7 0.2 fusion.38
  91.0 9.5 %fusion.23 = f32[16,8,128]{2,1,0:T(8,128)S(1)} fusion(f32[16,128,128]{2,1,0:T(8,128)} %convert_multiply_fusion.2, f32[16,8,128]{2,1,0:T(8,128)S(1)} %copy.42, f32[16,8,128]{2,1,0:T(8,128)S(1)} %copy.40), kind=kLoop, calls=%fused_computation.33 | loop fusion | flops 25149440 | bytes 1245184 | tf_op jit(solution)/shard_map/while/body/eval_jaxpr/reduce_sum | solution.py:99
  100.4 0.1 convolution_bitcast_fusion.2
  100.7 11.2 %reshape.149 = bf16[32,128,8,64]{3,2,1,0:T(8,128)(2,1)} reshape(bf16[4096,512]{1,0:T(8,128)(2,1)} %all-gather.2.cloned.1.call-done) | data formatting | bytes 8388608 | tf_op jit(solution)/shard_map/reshape;reshape | solution.py:55
  111.8 9.1 %copy.47 = bf16[32,128,8,64]{1,3,2,0:T(8,128)(2,1)} copy(bf16[32,128,8,64]{3,2,1,0:T(8,128)(2,1)} %reshape.149) | data formatting | bytes 8388608 | tf_op jit(solution)/shard_map/reshape;reshape | solution.py:55
  120.9 4.3 gather_fusion.1
  125.3 9.9 %fusion.27 = f32[16,128,8,64]{1,3,2,0:T(8,128)S(1)} fusion(f32[16,128,128]{2,1,0:T(8,128)} %convert_multiply_fusion.2, f32[16,8,128]{2,1,0:T(8,128)S(1)} %copy.42, f32[16,8,128]{2,1,0:T(8,128)S(1)} %copy.40, bf16[16,128,8,64]{1,3,2,0:T(8,128)(2,1)} %gather_fusion.1, pred[16]{0:T(512)(128)(4,1)S(1)} %get-tuple-element.104), kind=kOutput, calls=%fused_computation.35 | convolution fusion | flops 294649856 | bytes 7471120 | tf_op jit(solution)/shard_map/while/body/eval_jaxpr/ghij,gjhk->gihk/dot_general | solution.py:92
  135.1 5.0 fusion.14
  140.1 2.6 reshape.108
  142.8 1.6 fusion.33
  144.4 0.2 fusion.89
  144.6 0.2 fusion.91
  144.9 11.8 %fusion.24 = f32[16,128,8,64]{1,3,2,0:T(8,128)S(1)} fusion(f32[16,8,128]{2,1,0:T(8,128)S(1)} %copy.44, f32[16,128,128]{2,1,0:T(8,128)} %convert_multiply_fusion.2, f32[16,8,128]{2,1,0:T(8,128)S(1)} %copy.42, f32[16,8,128]{2,1,0:T(8,128)S(1)} %copy.40, bf16[16,128,8,64]{1,3,2,0:T(8,128)(2,1)S(1)} %gather_fusion, pred[16]{0:T(512)(128)(4,1)S(1)} %get-tuple-element.105), kind=kOutput, calls=%fused_computation.34 | convolution fusion | flops 296747008 | bytes 7536656 | tf_op jit(solution)/shard_map/while/body/eval_jaxpr/ghij,gihk->gjhk/dot_general | solution.py:143
  156.7 15.4 %fusion.96 = (f32[16,8,128]{2,1,0:T(8,128)S(1)}, f32[16,8,128]{2,1,0:T(8,128)S(1)}) fusion(f32[16,8,128]{2,1,0:T(8,128)S(1)} %copy.50, bf16[16,128,8,64]{1,3,2,0:T(8,128)(2,1)S(1)} %copy-done.1, pred[16]{0:T(512)(128)(4,1)S(1)} %get-tuple-element.104, bf16[16,128,8,64]{1,3,2,0:T(8,128)(2,1)S(1)} %gather_fusion, pred[16]{0:T(512)(128)(4,1)S(1)} %get-tuple-element.105, ...), kind=kOutput, calls=%fused_computation.128 | convolution fusion | flops 316637184 | bytes 5636128 | tf_op jit(solution)/shard_map/while/body/eval_jaxpr/gihk,gjhk->ghij/dot_general | solution.py:136
  172.2 0.3 fusion.42
  172.5 0.1 copy.112
  172.6 5.8 fusion.16
  178.4 12.0 %bitcast_add_fusion = f32[4096,512]{0,1:T(8,128)} fusion(f32[64,8,32,128]{3,2,1,0:T(8,128)S(1)} %bitcast.176, f32[512]{0:T(512)S(1)} %mul.185, f32[4096,8]{0,1:T(8,128)S(1)} %bitcast.183), kind=kLoop, calls=%fused_computation.22 | loop fusion | flops 4194304 | bytes 16910336 | tf_op jit(solution)/shard_map/add | solution.py:181
  190.4 0.0 reduce-scatter.2.cloned.1.call-update
  190.5 0.0 all-reduce.4.cloned.1.call-start
  190.5 0.6 copy-done.8
  191.1 0.1 mul.201
  191.2 0.1 convolution_bitcast_fusion.1
  191.4 0.1 copy-done.3
  191.5 0.3 fusion.34
  191.8 0.5 fusion.59
  192.3 0.6 convolution_bitcast_fusion
  192.9 5.1 fusion.103
  198.0 122.5 %reduce-scatter.2.cloned.1.call-done = f32[128,512]{0,1:T(8,128)} async-done(((f32[4096,512]{0,1:T(8,128)}), f32[128,512]{0,1:T(8,128)}) %reduce-scatter.2.cloned.1.call-update) | async-done | bytes 262160 | tf_op jit(solution)/shard_map/reduce_scatter | solution.py:193
  320.5 0.0 all-reduce.4.cloned.1.call-update
  320.5 0.0 all-reduce.6.cloned.1.call-start
  320.5 0.5 fusion.57
  321.0 75.9 %all-reduce = (f32[8,64]{1,0:T(8,128)}, f32[8,64]{1,0:T(8,128)}) all-reduce(f32[8,64]{1,0:T(8,128)S(1)} %add.168, f32[8,64]{1,0:T(8,128)S(1)} %bitcast.197), channel_id=1, replica_groups=mesh['panel'=32,'rep'=8] {'panel','rep'}, use_global_device_ids=true, to_apply=%region_8.10 | all-reduce | flops 1024 | bytes 8192 | tf_op jit(solution)/shard_map/psum | solution.py:199
  396.9 1.7 fusion.102
  398.6 11.2 %all-reduce.4.cloned.1.call-done = f32[128,512]{0,1:T(8,128)} async-done(((f32[128,512]{0,1:T(8,128)}), f32[128,512]{0,1:T(8,128)}) %all-reduce.4.cloned.1.call-update) | async-done | bytes 262160 | tf_op jit(solution)/shard_map/psum | solution.py:194
  409.9 2.0 convolution_add_fusion
  411.9 0.0 all-reduce.6.cloned.1.call-update
  411.9 2.0 fusion.101
  413.8 252.2 %all-reduce.6.cloned.1.call-done = f32[128,512]{0,1:T(8,128)} async-done(((f32[128,512]{0,1:T(8,128)}), f32[128,512]{0,1:T(8,128)}) %all-reduce.6.cloned.1.call-update) | async-done | bytes 262160 | tf_op jit(solution)/shard_map/psum | solution.py:199
  666.1 1.8 copy.54
  (31 shorter events, 0.3 us)
Async XLA Ops:
  7.2 0.9 copy-start
  7.2 13.2 %copy-start.7 = (s32[16]{0:T(128)S(1)}, s32[16]{0:T(128)}, u32[]{:S(2)}) copy-start(s32[16]{0:T(128)} %param.18) | copy-start | bytes 196
  7.2 13.2 %copy-start.6 = (f32[8,64]{1,0:T(8,128)S(1)}, f32[8,64]{1,0:T(8,128)}, u32[]{:S(2)}) copy-start(f32[8,64]{1,0:T(8,128)} %param.15) | copy-start | bytes 6148
  7.2 13.1 %copy-start.9 = (s32[16]{0:T(128)S(1)}, s32[16]{0:T(128)}, u32[]{:S(2)}) copy-start(s32[16]{0:T(128)} %param.19) | copy-start | bytes 196
  7.2 73.1 %all-gather.2.cloned.1.call-start = ((), (), s32[]{:S(2)}) async-start(), calls=%async_computation.1 | async-start | bytes 4325376 | tf_op jit(solution)/shard_map/all_gather | solution.py:37
  9.7 310.8 %reduce-scatter.2.cloned.1.call-start = ((), (), s32[]{:S(2)}) async-start(), calls=%async_computation.2 | async-start | bytes 8650752 | tf_op jit(solution)/shard_map/reduce_scatter | solution.py:193
  125.2 17.5 %copy-start.2 = (bf16[512,512]{0,1:T(8,128)(2,1)S(1)}, bf16[512,512]{0,1:T(8,128)(2,1)}, u32[]{:S(2)}) copy-start(bf16[512,512]{0,1:T(8,128)(2,1)} %copy.48) | copy-start | bytes 1572868
  144.9 11.8 %copy-start.1 = (bf16[16,128,8,64]{1,3,2,0:T(8,128)(2,1)S(1)}, bf16[16,128,8,64]{1,3,2,0:T(8,128)(2,1)}, u32[]{:S(2)}) copy-start(bf16[16,128,8,64]{1,3,2,0:T(8,128)(2,1)} %gather_fusion.1) | copy-start | bytes 6291460
  144.9 11.8 %copy-start.4 = (f32[16,128,128]{2,1,0:T(8,128)S(1)}, f32[16,128,128]{2,1,0:T(8,128)}, u32[]{:S(2)}) copy-start(f32[16,128,128]{2,1,0:T(8,128)} %convert_multiply_fusion.2) | copy-start | bytes 3145732
  190.4 0.7 copy-start.8
  190.4 1.1 copy-start.3
  190.4 1.8 copy-start.5
  190.5 219.4 %all-reduce.4.cloned.1.call-start = ((), (), s32[]{:S(2)}) async-start(), calls=%async_computation.3 | async-start | bytes 524288 | tf_op jit(solution)/shard_map/psum | solution.py:194
  320.5 345.6 %all-reduce.6.cloned.1.call-start = ((), (), s32[]{:S(2)}) async-start(), calls=%async_computation.4 | async-start | bytes 524288 | tf_op jit(solution)/shard_map/psum | solution.py:199
Sparse Core Ops, SparseCore 0:
  10.5 69.7 all-gather.1
  190.6 129.8 reduce-scatter.1
  323.1 86.7 all-reduce.3
  416.6 249.4 all-reduce.5
where the time goes:
time: 682 us; the launch traced here: 675 us
  waiting for transfers between devices  443 us (65%)
  blocking collectives  75.9 us (11%)
  matrix products  70.5 us (10%)
  local copies, waits for them, and re-layouts  43.3 us (6%)
  other arithmetic  26.5 us (4%)
  between operations  15 us (2%)
    psum x1, waiting for transfers between devices, shards(): lax.psum((weight_part, att_src_part, att_dst_part), ('panel', 'rep'))  252 us
    reduce_scatter x1, waiting for transfers between devices, shards(): lax.psum_scatter(source_flat, 'panel', scatter_dimension=0, tiled=True)  122 us
    psum x1, blocking collectives, shards(): lax.psum((weight_part, att_src_part, att_dst_part), ('panel', 'rep'))  75.9 us
    all_gather x1, waiting for transfers between devices, shards(): proj_all = lax.all_gather(proj_own, 'panel', axis=0, tiled=True)  57.2 us
    another operation x2, local copies, waits for them, and re-layouts, shards(): source_feats.reshape(source_blocks, block_size, num_heads, head_dim)  20.2 us
    dot_general x1, matrix products, backward_group(): jnp.einsum('gihk,gjhk->ghij', cotan_rows, source_rows, preferred_element_...  15.4 us
  transfers between devices with their start and end apart: 4, of which 4 were waited for; matrix products, arithmetic and copies ran while one was open for 3% of the time, Pallas kernels for 0%

commit v1 on v0

--- a/solution.py
+++ b/solution.py
@@ -197,7 +197,7 @@
     own_inputs = lax.dynamic_slice_in_dim(x_src, share_start, share_rows, 0).astype(jnp.float32)
     weight_part = weight_part + jnp.dot(own_inputs.T, own_share, precision=HIGHEST_PRECISION)
     grad_weight, grad_att_src, grad_att_dst = lax.psum(
-        (weight_part, att_src_part, att_dst_part), ("panel", "rep")
+        lax.psum((weight_part, att_src_part, att_dst_part), "rep"), "panel"
     )
     return (grad_src, grad_dst, grad_weight, grad_att_src, grad_att_dst)
 

time: 682 us -> 735 us (1.078)
  waiting for transfers between devices: 443 us -> 503 us
    psum x1, waiting for transfers between devices: 11.2 us -> 88.1 us  [shards(): panel_sum = lax.psum(panel_part, 'rep')]
    psum x1 -> x2, waiting for transfers between devices: 252 us -> 233 us  [the longest x1 147 us: shards(): lax.psum(lax.psum((weight_part, att_src_part, att_dst_part), 'rep'), 'pan...]
    psum x1 -> x2, blocking collectives: 75.9 us -> 74.3 us  [the longest x1 54.6 us: shards(): lax.psum(lax.psum((weight_part, att_src_part, att_dst_part), 'rep'), 'pan...]
  transfers between devices with their start and end apart: 4 -> 5, of which waited for: 4 -> 5; matrix products, arithmetic and copies ran while one was open for 3% -> 3% of each run, Pallas kernels for 0% -> 0%
where the time goes in v1:
time: 735 us; the launch traced here: 732 us
  waiting for transfers between devices  503 us (68%)
  blocking collectives  74.3 us (10%)
  matrix products  70.3 us (10%)
  local copies, waits for them, and re-layouts  43.3 us (6%)
  other arithmetic  26.6 us (4%)
  between operations  14.8 us (2%)
    psum x1, waiting for transfers between devices, shards(): lax.psum(lax.psum((weight_part, att_src_part, att_dst_part), 'rep'), 'pan...  147 us
    reduce_scatter x1, waiting for transfers between devices, shards(): lax.psum_scatter(source_flat, 'panel', scatter_dimension=0, tiled=True)  124 us
    psum x1, waiting for transfers between devices, shards(): panel_sum = lax.psum(panel_part, 'rep')  88.1 us
    psum x1, waiting for transfers between devices, shards(): lax.psum((weight_part, att_src_part, att_dst_part), 'rep')  86.2 us
    all_gather x1, waiting for transfers between devices, shards(): proj_all = lax.all_gather(proj_own, 'panel', axis=0, tiled=True)  57.2 us
    psum x1, blocking collectives, shards(): lax.psum(lax.psum((weight_part, att_src_part, att_dst_part), 'rep'), 'pan...  54.6 us
    another operation x2, local copies, waits for them, and re-layouts, shards(): source_feats.reshape(source_blocks, block_size, num_heads, head_dim)  20.2 us
    psum x1, blocking collectives, shards(): lax.psum((weight_part, att_src_part, att_dst_part), 'rep')  19.7 us
  transfers between devices with their start and end apart: 5, of which 5 were waited for; matrix products, arithmetic and copies ran while one was open for 3% of the time, Pallas kernels for 0%

profile of v1, /device:TPU:2, one launch (start us, length us, event | category | flops | bytes accessed | tf_op | source)
XLA Modules:
  0.0 732.1 jit_solution(6419881901970289395)
XLA Ops:
  7.2 0.0 copy-start
  7.2 0.0 all-gather.2.cloned.1.call-start
  7.3 0.8 copy-done
  8.1 1.6 convolution_convert_fusion.1
  9.7 0.0 all-gather.2.cloned.1.call-update
  9.7 0.0 reduce-scatter.2.cloned.1.call-start
  9.7 2.1 copy.48
  11.8 1.6 reshape.148
  13.5 1.2 convolution_convert_fusion
  14.7 1.0 fusion.98
  15.7 0.9 fusion.94
  17.3 0.6 copy.39
  17.9 0.8 mul.185
  18.7 0.7 compare_select_fusion.3
  19.4 0.9 gather_fusion
  20.4 0.3 fusion.100
  20.7 2.4 convert_multiply_fusion.2
  23.1 57.2 %all-gather.2.cloned.1.call-done = bf16[4096,512]{1,0:T(8,128)(2,1)} async-done(((bf16[128,512]{1,0:T(8,128)(2,1)}), bf16[4096,512]{1,0:T(8,128)(2,1)}) %all-gather.2.cloned.1.call-update) | async-done | bytes 4194320 | tf_op jit(solution)/shard_map/all_gather | solution.py:37
  80.3 6.4 copy.41
  86.7 3.9 fusion.99
  90.6 0.1 copy.113
  90.7 0.2 fusion.38
  91.0 9.5 %fusion.23 = f32[16,8,128]{2,1,0:T(8,128)S(1)} fusion(f32[16,128,128]{2,1,0:T(8,128)} %convert_multiply_fusion.2, f32[16,8,128]{2,1,0:T(8,128)S(1)} %copy.42, f32[16,8,128]{2,1,0:T(8,128)S(1)} %copy.40), kind=kLoop, calls=%fused_computation.33 | loop fusion | flops 25149440 | bytes 1245184 | tf_op jit(solution)/shard_map/while/body/eval_jaxpr/reduce_sum | solution.py:99
  100.4 0.1 convolution_bitcast_fusion.2
  100.7 11.2 %reshape.149 = bf16[32,128,8,64]{3,2,1,0:T(8,128)(2,1)} reshape(bf16[4096,512]{1,0:T(8,128)(2,1)} %all-gather.2.cloned.1.call-done) | data formatting | bytes 8388608 | tf_op jit(solution)/shard_map/reshape;reshape | solution.py:55
  111.8 9.0 %copy.47 = bf16[32,128,8,64]{1,3,2,0:T(8,128)(2,1)} copy(bf16[32,128,8,64]{3,2,1,0:T(8,128)(2,1)} %reshape.149) | data formatting | bytes 8388608 | tf_op jit(solution)/shard_map/reshape;reshape | solution.py:55
  120.9 4.4 gather_fusion.1
  125.2 9.6 %fusion.27 = f32[16,128,8,64]{1,3,2,0:T(8,128)S(1)} fusion(f32[16,128,128]{2,1,0:T(8,128)} %convert_multiply_fusion.2, f32[16,8,128]{2,1,0:T(8,128)S(1)} %copy.42, f32[16,8,128]{2,1,0:T(8,128)S(1)} %copy.40, bf16[16,128,8,64]{1,3,2,0:T(8,128)(2,1)} %gather_fusion.1, pred[16]{0:T(512)(128)(4,1)S(1)} %get-tuple-element.106), kind=kOutput, calls=%fused_computation.35 | convolution fusion | flops 294649856 | bytes 7471120 | tf_op jit(solution)/shard_map/while/body/eval_jaxpr/ghij,gjhk->gihk/dot_general | solution.py:92
  134.8 5.0 fusion.14
  139.9 2.6 reshape.108
  142.5 1.6 fusion.33
  144.1 0.2 fusion.89
  144.4 0.2 fusion.91
  144.7 11.8 %fusion.24 = f32[16,128,8,64]{1,3,2,0:T(8,128)S(1)} fusion(f32[16,8,128]{2,1,0:T(8,128)S(1)} %copy.44, f32[16,128,128]{2,1,0:T(8,128)} %convert_multiply_fusion.2, f32[16,8,128]{2,1,0:T(8,128)S(1)} %copy.42, f32[16,8,128]{2,1,0:T(8,128)S(1)} %copy.40, bf16[16,128,8,64]{1,3,2,0:T(8,128)(2,1)S(1)} %gather_fusion, pred[16]{0:T(512)(128)(4,1)S(1)} %get-tuple-element.107), kind=kOutput, calls=%fused_computation.34 | convolution fusion | flops 296747008 | bytes 7536656 | tf_op jit(solution)/shard_map/while/body/eval_jaxpr/ghij,gihk->gjhk/dot_general | solution.py:143
  156.5 15.5 %fusion.96 = (f32[16,8,128]{2,1,0:T(8,128)S(1)}, f32[16,8,128]{2,1,0:T(8,128)S(1)}) fusion(f32[16,8,128]{2,1,0:T(8,128)S(1)} %copy.50, bf16[16,128,8,64]{1,3,2,0:T(8,128)(2,1)S(1)} %copy-done.1, pred[16]{0:T(512)(128)(4,1)S(1)} %get-tuple-element.106, bf16[16,128,8,64]{1,3,2,0:T(8,128)(2,1)S(1)} %gather_fusion, pred[16]{0:T(512)(128)(4,1)S(1)} %get-tuple-element.107, ...), kind=kOutput, calls=%fused_computation.128 | convolution fusion | flops 316637184 | bytes 5636128 | tf_op jit(solution)/shard_map/while/body/eval_jaxpr/gihk,gjhk->ghij/dot_general | solution.py:136
  172.0 0.3 fusion.42
  172.3 0.1 copy.112
  172.4 5.8 fusion.16
  178.2 12.1 %bitcast_add_fusion = f32[4096,512]{0,1:T(8,128)} fusion(f32[64,8,32,128]{3,2,1,0:T(8,128)S(1)} %bitcast.176, f32[512]{0:T(512)S(1)} %mul.185, f32[4096,8]{0,1:T(8,128)S(1)} %bitcast.183), kind=kLoop, calls=%fused_computation.22 | loop fusion | flops 4194304 | bytes 16910336 | tf_op jit(solution)/shard_map/add | solution.py:181
  190.3 0.0 reduce-scatter.2.cloned.1.call-update
  190.3 0.0 all-reduce.6.cloned.1.call-start
  190.4 0.6 copy-done.8
  191.0 0.1 mul.201
  191.1 0.1 convolution_bitcast_fusion.1
  191.2 5.1 fusion.103
  196.3 124.2 %reduce-scatter.2.cloned.1.call-done = f32[128,512]{0,1:T(8,128)} async-done(((f32[4096,512]{0,1:T(8,128)}), f32[128,512]{0,1:T(8,128)}) %reduce-scatter.2.cloned.1.call-update) | async-done | bytes 262160 | tf_op jit(solution)/shard_map/reduce_scatter | solution.py:193
  320.5 0.0 all-reduce.6.cloned.1.call-update
  320.5 0.0 all-reduce.8.cloned.1.call-start
  320.6 0.3 fusion.34
  320.9 0.6 convolution_bitcast_fusion
  321.5 88.1 %all-reduce.6.cloned.1.call-done = f32[128,512]{0,1:T(8,128)} async-done(((f32[128,512]{0,1:T(8,128)}), f32[128,512]{0,1:T(8,128)}) %all-reduce.6.cloned.1.call-update) | async-done | bytes 262160 | tf_op jit(solution)/shard_map/psum | solution.py:194
  409.6 2.0 convolution_add_fusion
  411.6 0.0 all-reduce.8.cloned.1.call-update
  411.6 0.0 all-reduce.10.cloned.1.call-start
  411.6 0.5 fusion.59
  412.2 1.7 fusion.102
  413.9 86.2 %all-reduce.8.cloned.1.call-done = f32[128,512]{0,1:T(8,128)} async-done(((f32[128,512]{0,1:T(8,128)}), f32[128,512]{0,1:T(8,128)}) %all-reduce.8.cloned.1.call-update) | async-done | bytes 262160 | tf_op jit(solution)/shard_map/psum | solution.py:200
  500.0 0.0 all-reduce.10.cloned.1.call-update
  500.1 0.5 fusion.57
  500.6 19.7 %all-reduce.1 = (f32[8,64]{1,0:T(8,128)S(1)}, f32[8,64]{1,0:T(8,128)S(1)}) all-reduce(f32[8,64]{1,0:T(8,128)S(1)} %add.174, f32[8,64]{1,0:T(8,128)S(1)} %bitcast.197), channel_id=1, replica_groups=mesh['panel'=32,'rep'=8] {'rep'}, use_global_device_ids=true, to_apply=%region_9.11 | all-reduce | flops 1024 | bytes 8192 | tf_op jit(solution)/shard_map/psum | solution.py:200
  520.3 54.6 %all-reduce = (f32[8,64]{1,0:T(8,128)}, f32[8,64]{1,0:T(8,128)}) all-reduce(f32[8,64]{1,0:T(8,128)S(1)} %get-tuple-element.99, f32[8,64]{1,0:T(8,128)S(1)} %get-tuple-element.100), channel_id=1, replica_groups=mesh['panel'=32,'rep'=8] {'panel'}, use_global_device_ids=true, to_apply=%region_10.12 | all-reduce | flops 1024 | bytes 8192 | tf_op jit(solution)/shard_map/psum | solution.py:199
  574.9 2.0 fusion.101
  576.9 146.9 %all-reduce.10.cloned.1.call-done = f32[128,512]{0,1:T(8,128)} async-done(((f32[128,512]{0,1:T(8,128)}), f32[128,512]{0,1:T(8,128)}) %all-reduce.10.cloned.1.call-update) | async-done | bytes 262160 | tf_op jit(solution)/shard_map/psum | solution.py:199
  723.8 1.8 copy.54
  (35 shorter events, 0.3 us)
Async XLA Ops:
  7.2 0.9 copy-start
  7.2 13.2 %copy-start.7 = (s32[16]{0:T(128)S(1)}, s32[16]{0:T(128)}, u32[]{:S(2)}) copy-start(s32[16]{0:T(128)} %param.18) | copy-start | bytes 196
  7.2 13.2 %copy-start.6 = (f32[8,64]{1,0:T(8,128)S(1)}, f32[8,64]{1,0:T(8,128)}, u32[]{:S(2)}) copy-start(f32[8,64]{1,0:T(8,128)} %param.15) | copy-start | bytes 6148
  7.2 13.1 %copy-start.9 = (s32[16]{0:T(128)S(1)}, s32[16]{0:T(128)}, u32[]{:S(2)}) copy-start(s32[16]{0:T(128)} %param.19) | copy-start | bytes 196
  7.2 73.1 %all-gather.2.cloned.1.call-start = ((), (), s32[]{:S(2)}) async-start(), calls=%async_computation.1 | async-start | bytes 4325376 | tf_op jit(solution)/shard_map/all_gather | solution.py:37
  9.7 310.8 %reduce-scatter.2.cloned.1.call-start = ((), (), s32[]{:S(2)}) async-start(), calls=%async_computation.2 | async-start | bytes 8650752 | tf_op jit(solution)/shard_map/reduce_scatter | solution.py:193
  125.2 17.3 %copy-start.2 = (bf16[512,512]{0,1:T(8,128)(2,1)S(1)}, bf16[512,512]{0,1:T(8,128)(2,1)}, u32[]{:S(2)}) copy-start(bf16[512,512]{0,1:T(8,128)(2,1)} %copy.48) | copy-start | bytes 1572868
  144.6 11.8 %copy-start.1 = (bf16[16,128,8,64]{1,3,2,0:T(8,128)(2,1)S(1)}, bf16[16,128,8,64]{1,3,2,0:T(8,128)(2,1)}, u32[]{:S(2)}) copy-start(bf16[16,128,8,64]{1,3,2,0:T(8,128)(2,1)} %gather_fusion.1) | copy-start | bytes 6291460
  144.7 11.8 %copy-start.4 = (f32[16,128,128]{2,1,0:T(8,128)S(1)}, f32[16,128,128]{2,1,0:T(8,128)}, u32[]{:S(2)}) copy-start(f32[16,128,128]{2,1,0:T(8,128)} %convert_multiply_fusion.2) | copy-start | bytes 3145732
  190.3 0.7 copy-start.8
  190.3 130.3 %copy-start.3 = (bf16[512,512]{0,1:T(8,128)(2,1)S(1)}, bf16[512,512]{0,1:T(8,128)(2,1)}, u32[]{:S(2)}) copy-start(bf16[512,512]{0,1:T(8,128)(2,1)} %copy.48) | copy-start | bytes 1572868
  190.3 130.6 %copy-start.5 = (bf16[512,128]{1,0:T(8,128)(2,1)S(1)}, bf16[512,128]{1,0:T(8,128)(2,1)}, u32[]{:S(2)}) copy-start(bf16[512,128]{1,0:T(8,128)(2,1)} %param.13) | copy-start | bytes 393220
  190.3 219.3 %all-reduce.6.cloned.1.call-start = ((), (), s32[]{:S(2)}) async-start(), calls=%async_computation.3 | async-start | bytes 524288 | tf_op jit(solution)/shard_map/psum | solution.py:194
  320.5 179.5 %all-reduce.8.cloned.1.call-start = ((), (), s32[]{:S(2)}) async-start(), calls=%async_computation.4 | async-start | bytes 524288 | tf_op jit(solution)/shard_map/psum | solution.py:200
  411.6 312.2 %all-reduce.10.cloned.1.call-start = ((), (), s32[]{:S(2)}) async-start(), calls=%async_computation.5 | async-start | bytes 524288 | tf_op jit(solution)/shard_map/psum | solution.py:199
Sparse Core Ops, SparseCore 0:
  10.5 69.7 all-gather.1
  190.4 130.0 reduce-scatter.1
  323.1 86.3 all-reduce.5
  412.8 87.1 all-reduce.7
  502.5 221.2 all-reduce.9
